TPU v7x, 32 devices: a whole 2x2x4 slice. The times are simulated.
32 devices in a mesh: groups: 2 (over y), feat: 4 (over z), dp: 2 (over x), rep: 2 (over core).
Axes of the slice: x: 2, y: 2, z: 4, core: 2. Of those that a mesh axis runs over, the one named last changes fastest.
Arguments:
- tokens: bfloat16 [4096, 16384], P(('groups', 'dp', 'rep'), 'feat'), parts along dimension 0, may hold values from -6 to 6
- cotangent: bfloat16 [4096, 16384], P(('groups', 'dp', 'rep'), 'feat'), parts along dimension 0, may hold values from -6 to 6
- mix_first: bfloat16 [128, 2, 128, 128], P('feat'), may hold values from -0.375 to 0.375
- up_weight: bfloat16 [128, 128, 512], P('feat'), may hold values from -0.5 to 0.5
- down_weight: bfloat16 [128, 512, 128], P('feat'), may hold values from -0.25 to 0.25
- mix_second: bfloat16 [128, 2, 128, 128], P('feat'), may hold values from -0.375 to 0.375
- order: int32 [128], P('feat'), may hold values from 0 to 31, as said below
Outputs:
- grad_tokens: bfloat16 [4096, 16384], P(('groups', 'dp', 'rep'), 'feat'), parts along dimension 0
- grad_first: float32 [256, 2, 128, 128], P(('groups', 'feat'), None, ('dp', 'rep')), parts along dimension 0
- grad_up: float32 [256, 128, 512], P(('groups', 'feat'), ('dp', 'rep')), parts along dimension 0
- grad_down: float32 [256, 512, 128], P(('groups', 'feat'), ('dp', 'rep')), parts along dimension 0
- grad_second: float32 [256, 2, 128, 128], P(('groups', 'feat'), None, ('dp', 'rep')), parts along dimension 0
There are 2 independent parts, one for each index of `groups`. A program takes and returns all parts, laid end to end along the dimension named above; an argument that names none is the same for every part. Nothing has to cross between parts.
Inputs may be any that keep to these rules, and one draw needn't show every extreme that they name: `order`: each aligned run of 32 entries (the blocks of one index of feat) is a permutation of 0 to 31.
All inputs are finite; a program needn't handle non-finite values.
Results may differ from a plain program's by a relative error of at most 0.0095.
Values may be sent and summed in bfloat16 or wider, within the bound.
A program may use at most 256 MiB of HBM per device.

v0:
```python
import functools

import jax
import jax.numpy as jnp
from jax import lax
from jax.experimental import pallas as pl
from jax.experimental.pallas import tpu as pltpu
from jax.sharding import PartitionSpec as P


GELU_C = 0.7978845608028654
GELU_K = 0.044715
SHARES = (1, 1, 2)


def swapped(x, axis, bit):
    return lax.ppermute(x, axis, [(i, i ^ 1 << bit) for i in range(lax.axis_size(axis))])


def dot(left, right, dims):
    return lax.dot_general(left, right, (dims, ((), ())), preferred_element_type=jnp.float32)


NN = ((1,), (0,))
NT = ((1,), (1,))
TN = ((0,), (0,))


def block_kernel(has_prev, order_ref, x_ref, xf_ref, c_ref, cn_ref, mix_ref, up_ref, down_ref, p_ref, q_ref, *rest):
    if has_prev:
        prev, rest = rest[:4], rest[4:]
    else:
        prev = None
    r_ref, dx_ref, gf_ref, gu_ref, gd_ref, gs_ref = rest
    width = x_ref.shape[1]

    def emit(ref, which, value, index):
        if prev is not None:
            value = value + prev[which][index].astype(jnp.float32)
        ref[index] = value.astype(ref.dtype)

    x2 = jnp.concatenate([x_ref[...], xf_ref[...]], axis=1)
    c2 = jnp.concatenate([c_ref[...], cn_ref[...]], axis=1)
    mix = mix_ref[0].reshape(2 * width, width)
    pq = jnp.concatenate([p_ref[0, 0], q_ref[0]], axis=1)
    up = up_ref[0]
    down = down_ref[0]
    v = dot(x2, mix, NN).astype(jnp.bfloat16)
    dz = dot(c2, pq, NT).astype(jnp.bfloat16)
    h = dot(v, up, NN)
    da = dot(dz, down, NT)
    h2 = h * h
    t = jnp.tanh(h * (GELU_C + (GELU_C * GELU_K) * h2))
    p = 0.5 + 0.5 * t
    act = h * p
    slope = p + act * (1.0 - p) * (2.0 * GELU_C + (6.0 * GELU_C * GELU_K) * h2)
    a = act.astype(jnp.bfloat16)
    dh = (da * slope).astype(jnp.bfloat16)
    z = dot(a, down, NN).astype(jnp.bfloat16)
    du = dot(dh, up, NT).astype(jnp.bfloat16)
    both = dot(du, mix, NT)
    dx_ref[...] = both[:, :width]
    r_ref[...] = both[:, width:].astype(jnp.bfloat16)
    gf = dot(x2, du, TN)
    emit(gf_ref, 0, gf[:width], (0, 0))
    emit(gf_ref, 0, gf[width:], (0, 1))
    emit(gu_ref, 1, dot(v, dh, TN), 0)
    emit(gd_ref, 2, dot(a, dz, TN), 0)
    gs = dot(z, c2, TN)
    emit(gs_ref, 3, gs[:, :width], (0, 0))
    emit(gs_ref, 3, gs[:, width:], (0, 1))


def process(offset, rows, order, tokens, far_in, cotangent, near_in, mix_first, up, down, mix_second, near_q, prev):
    blocks, _, width, _ = mix_first.shape
    hidden = up.shape[2]
    at_source = lambda b, o: (0, o[b])
    act_spec = lambda m: pl.BlockSpec((rows, width), m)
    first_spec = pl.BlockSpec((1, 2, width, width), lambda b, o: (o[b], 0, 0, 0))
    up_spec = pl.BlockSpec((1, width, hidden), lambda b, o: (b, 0, 0))
    down_spec = pl.BlockSpec((1, hidden, width), lambda b, o: (b, 0, 0))
    second_spec = pl.BlockSpec((1, 2, width, width), lambda b, o: (b, 0, 0, 0))
    grad_specs = [first_spec, up_spec, down_spec, second_spec]
    in_specs = [
        act_spec(lambda b, o: (offset // rows, o[b])),
        act_spec(at_source),
        act_spec(lambda b, o: (offset // rows, b)),
        act_spec(lambda b, o: (0, b)),
        first_spec,
        up_spec,
        down_spec,
        pl.BlockSpec((1, 1, width, width), lambda b, o: (b, 0, 0, 0)),
        pl.BlockSpec((1, width, width), lambda b, o: (b, 0, 0)),
    ]
    operands = [tokens, far_in, cotangent, near_in, mix_first, up, down, mix_second, near_q]
    if prev is not None:
        in_specs += grad_specs
        operands += prev
    bf = jnp.bfloat16
    out_shape = [
        jax.ShapeDtypeStruct((rows, blocks * width), bf),
        jax.ShapeDtypeStruct((rows, blocks * width), jnp.float32),
        jax.ShapeDtypeStruct(mix_first.shape, bf),
        jax.ShapeDtypeStruct(up.shape, bf),
        jax.ShapeDtypeStruct(down.shape, bf),
        jax.ShapeDtypeStruct(mix_second.shape, bf),
    ]
    macs = rows * blocks * width * (10 * width + 6 * hidden)
    out = pl.pallas_call(
        functools.partial(block_kernel, prev is not None),
        grid_spec=pltpu.PrefetchScalarGridSpec(
            num_scalar_prefetch=1,
            grid=(blocks,),
            in_specs=in_specs,
            out_specs=[act_spec(at_source), act_spec(at_source)] + grad_specs,
        ),
        out_shape=out_shape,
        compiler_params=pltpu.CompilerParams(dimension_semantics=("arbitrary",)),
        cost_estimate=pl.CostEstimate(
            flops=4 * macs,
            bytes_accessed=60 * 2**20,
            transcendentals=rows * blocks * hidden,
        ),
    )(order, *operands)
    return out[0], out[1], list(out[2:])


def summed(parts, row_dim):
    stages = [("rep", bit) for bit in range(lax.axis_size("rep").bit_length() - 1)]
    dp_bits = lax.axis_size("dp").bit_length() - 1
    rep_bits = len(stages)
    stages += [("dp", bit) for bit in reversed(range(dp_bits))]
    shape = parts.shape
    owners = 1 << (dp_bits + rep_bits)
    names = [("dp", bit) for bit in reversed(range(dp_bits))]
    names += [("rep", bit) for bit in reversed(range(rep_bits))]
    x = parts.reshape(
        shape[:row_dim] + (2,) * len(names) + (shape[row_dim] // owners,) + shape[row_dim + 1 :]
    )
    for axis, bit in stages:
        where = row_dim + names.index((axis, bit))
        names.remove((axis, bit))
        mine = (lax.axis_index(axis) >> bit) & 1
        kept = lax.dynamic_index_in_dim(x, mine, where, keepdims=False)
        sent = lax.dynamic_index_in_dim(x, 1 - mine, where, keepdims=False)
        got = swapped(sent, axis, bit)
        x = kept.astype(jnp.float32) + got.astype(jnp.float32)
        if names:
            x = x.astype(jnp.bfloat16)
    return x


def neighbour_weights(weights):
    half = weights.shape[0] // 2
    side = lax.axis_index("rep")
    part = lax.dynamic_slice_in_dim(weights, side * half, half, axis=0)
    mine = swapped(part, "feat", 0)
    other = swapped(mine, "rep", 0)
    low = jnp.where(side == 0, mine, other)
    high = jnp.where(side == 0, other, mine)
    return jnp.concatenate([low, high], axis=0)


def per_device(tokens, cotangent, mix_first, up_weight, down_weight, mix_second, order):
    row_count = tokens.shape[0]
    top_bit = lax.axis_size("feat").bit_length() - 2
    sizes = [row_count * share // sum(SHARES) for share in SHARES]
    offsets = [sum(sizes[:i]) for i in range(len(sizes))]
    cut = lambda x, i: lax.slice_in_dim(x, offsets[i], offsets[i] + sizes[i], axis=0)
    far_in, near_in = [], []
    near_q = neighbour_weights(mix_second[:, 1])
    for i in range(len(sizes)):
        near_in.append(swapped(cut(cotangent, i), "feat", 0))
        far_in.append(swapped(cut(tokens, i), "feat", top_bit))
    grads = None
    backs, directs = [], []
    for i in range(len(sizes)):
        back, direct, grads = process(
            offsets[i], sizes[i], order, tokens, far_in[i], cotangent, near_in[i],
            mix_first, up_weight, down_weight, mix_second, near_q, grads,
        )
        backs.append(swapped(back, "feat", top_bit))
        directs.append(direct)
    first, up, down, second = grads
    second_sum = summed(second, 2)
    near_sum = swapped(second_sum[:, 1].astype(jnp.bfloat16), "feat", 0).astype(jnp.float32)
    second_sum = jnp.stack([second_sum[:, 0], near_sum], axis=1)
    up_sum = summed(up, 1)
    down_sum = summed(down, 1)
    first_sum = summed(first, 2)
    grad_inputs = jnp.concatenate(
        [
            (direct + back.astype(jnp.float32)).astype(jnp.bfloat16)
            for direct, back in zip(directs, backs)
        ],
        axis=0,
    )
    return grad_inputs, first_sum, up_sum, down_sum, second_sum


def solution(mesh):
    placed = (
        P(("groups", "dp", "rep"), "feat"),
        P(("groups", "dp", "rep"), "feat"),
        P("feat", None, None, None),
        P("feat", None, None),
        P("feat", None, None),
        P("feat", None, None, None),
        P("feat"),
    )

    return jax.shard_map(
        per_device,
        mesh=mesh,
        in_specs=placed,
        out_specs=(
            P(("groups", "dp", "rep"), "feat"),
            P(("groups", "feat"), None, ("dp", "rep"), None),
            P(("groups", "feat"), ("dp", "rep"), None),
            P(("groups", "feat"), ("dp", "rep"), None),
            P(("groups", "feat"), None, ("dp", "rep"), None),
        ),
        check_vma=False,
    )
```

profile of v0, /device:TPU:0, one launch (start us, length us, event | category | flops | bytes accessed | tf_op | source)
XLA Modules:
  0.0 428.1 jit_solution(14574071124221049591)
XLA Ops:
  1.9 3.1 collective-permute-start.2
  5.0 3.1 fusion.6
  8.1 2.6 collective-permute-start
  12.9 12.8 %collective-permute-done.2 = bf16[16,128,128]{2,1,0:T(8,128)(2,1)} collective-permute-done((bf16[16,128,128]{2,1,0:T(8,128)(2,1)S(1)}, bf16[16,128,128]{2,1,0:T(8,128)(2,1)}, u32[]{:S(2)}, u32[]{:S(2)}) %collective-permute-start.2) | collective-permute-done | bytes 524320 | tf_op jit(solution)/shard_map/ppermute | solution.py:17
  26.5 2.6 collective-permute-start.6
  29.1 1.9 slice.33
  33.4 24.6 %collective-permute-done.xf_ref = bf16[128,4096]{1,0:T(8,128)(2,1)} collective-permute-done((bf16[128,4096]{1,0:T(8,128)(2,1)}, bf16[128,4096]{1,0:T(8,128)(2,1)}, u32[]{:S(2)}, u32[]{:S(2)}) %collective-permute-start) | collective-permute-done | bytes 1048608 | tf_op jit(solution)/shard_map/ppermute | solution.py:17
  60.3 10.4 %collective-permute-done.1.cn_ref = bf16[128,4096]{1,0:T(8,128)(2,1)} collective-permute-done((bf16[128,4096]{1,0:T(8,128)(2,1)}, bf16[128,4096]{1,0:T(8,128)(2,1)}, u32[]{:S(2)}, u32[]{:S(2)}) %collective-permute-start.1) | collective-permute-done | bytes 1048608 | tf_op jit(solution)/shard_map/ppermute | solution.py:17
  70.7 34.2 %shard_map.110 = (bf16[128,4096]{1,0:T(8,128)(2,1)}, f32[128,4096]{1,0:T(8,128)}, bf16[32,2,128,128]{3,2,1,0:T(8,128)(2,1)}, bf16[32,128,512]{2,1,0:T(8,128)(2,1...) custom-call(s32[32]{0:T(128)} %order_ref.5, bf16[512,4096]{1,0:T(8,128)(2,1)} %x_ref.5, ...), custom_call_target="tpu_custom_call" | custom-call | flops 9126805504 | bytes 62914560 | tf_op jit(solution)/shard_map/pallas_call | solution.py:109
  105.8 54.8 %collective-permute-done.6.cn_ref = bf16[128,4096]{1,0:T(8,128)(2,1)} collective-permute-done((bf16[128,4096]{1,0:T(8,128)(2,1)}, bf16[128,4096]{1,0:T(8,128)(2,1)}, u32[]{:S(2)}, u32[]{:S(2)}) %collective-permute-start.6) | collective-permute-done | bytes 1048608 | tf_op jit(solution)/shard_map/ppermute | solution.py:17
  160.6 36.4 %shard_map.111 = (bf16[128,4096]{1,0:T(8,128)(2,1)}, f32[128,4096]{1,0:T(8,128)}, bf16[32,2,128,128]{3,2,1,0:T(8,128)(2,1)}, bf16[32,128,512]{2,1,0:T(8,128)(2,1...) custom-call(s32[32]{0:T(128)} %order_ref.5, bf16[512,4096]{1,0:T(8,128)(2,1)} %x_ref.5, ...), custom_call_target="tpu_custom_call" | custom-call | flops 9126805504 | bytes 62914560 | tf_op jit(solution)/shard_map/pallas_call | solution.py:109
  197.9 6.7 %collective-permute-done.9.cn_ref = bf16[256,4096]{1,0:T(8,128)(2,1)} collective-permute-done((bf16[256,4096]{1,0:T(8,128)(2,1)}, bf16[256,4096]{1,0:T(8,128)(2,1)}, u32[]{:S(2)}, u32[]{:S(2)}) %collective-permute-start.9) | collective-permute-done | bytes 2097184 | tf_op jit(solution)/shard_map/ppermute | solution.py:17
  204.7 41.1 %shard_map.112 = (bf16[256,4096]{1,0:T(8,128)(2,1)}, f32[256,4096]{1,0:T(8,128)}, bf16[32,2,128,128]{3,2,1,0:T(8,128)(2,1)}, bf16[32,128,512]{2,1,0:T(8,128)(2,1...) custom-call(s32[32]{0:T(128)} %order_ref.5, bf16[512,4096]{1,0:T(8,128)(2,1)} %x_ref.5, ...), custom_call_target="tpu_custom_call" | custom-call | flops 18253611008 | bytes 62914560 | tf_op jit(solution)/shard_map/pallas_call | solution.py:109
  246.4 3.6 constant_dynamic-slice_fusion.1
  255.4 49.7 %collective-permute-done.4 = bf16[128,4096]{1,0:T(8,128)(2,1)} collective-permute-done((bf16[128,4096]{1,0:T(8,128)(2,1)}, bf16[128,4096]{1,0:T(8,128)(2,1)}, u32[]{:S(2)}, u32[]{:S(2)}) %collective-permute-start.4) | collective-permute-done | bytes 1048608 | tf_op jit(solution)/shard_map/ppermute | solution.py:17
  307.5 20.0 %collective-permute-done.7 = bf16[128,4096]{1,0:T(8,128)(2,1)S(1)} collective-permute-done((bf16[128,4096]{1,0:T(8,128)(2,1)}, bf16[128,4096]{1,0:T(8,128)(2,1)S(1)}, u32[]{:S(2)}, u32[]{:S(2)}) %collective-permute-start.7) | collective-permute-done | bytes 1048608 | tf_op jit(solution)/shard_map/ppermute | solution.py:17
  330.2 12.0 %collective-permute-done.18 = bf16[32,2,32,128]{3,2,0,1:T(8,128)(2,1)S(1)} collective-permute-done((bf16[32,2,32,128]{3,2,0,1:T(8,128)(2,1)S(1)}, bf16[32,2,32,128]{3,2,0,1:T(8,128)(2,1)S(1)}, u32[]{:S(2)}, u32[]{:S(2)}) %collective-permute-start.18) | collective-permute-done | bytes 524320 | tf_op jit(solution)/shard_map/ppermute | solution.py:17
  342.6 7.3 %collective-permute-done.12 = bf16[32,2,32,128]{3,2,1,0:T(8,128)(2,1)S(1)} collective-permute-done((bf16[32,2,32,128]{3,2,1,0:T(8,128)(2,1)S(1)}, bf16[32,2,32,128]{3,2,1,0:T(8,128)(2,1)S(1)}, u32[]{:S(2)}, u32[]{:S(2)}) %collective-permute-start.12) | collective-permute-done | bytes 524320 | tf_op jit(solution)/shard_map/ppermute | solution.py:17
  351.1 25.6 %collective-permute-done.19 = bf16[32,32,128]{2,1,0:T(8,128)(2,1)S(1)} collective-permute-done((bf16[32,32,128]{2,1,0:T(8,128)(2,1)S(1)}, bf16[32,32,128]{2,1,0:T(8,128)(2,1)S(1)}, u32[]{:S(2)}, u32[]{:S(2)}) %collective-permute-start.19) | collective-permute-done | bytes 262176 | tf_op jit(solution)/shard_map/ppermute | solution.py:17
  383.0 2.3 pad_maximum_fusion
  385.3 19.5 %collective-permute-done.16 = bf16[32,128,128]{2,1,0:T(8,128)(2,1)S(1)} collective-permute-done((bf16[32,128,128]{2,1,0:T(8,128)(2,1)S(1)}, bf16[32,128,128]{2,1,0:T(8,128)(2,1)S(1)}, u32[]{:S(2)}, u32[]{:S(2)}) %collective-permute-start.16) | collective-permute-done | bytes 1048608 | tf_op jit(solution)/shard_map/ppermute | solution.py:17
  404.8 1.7 convert_add_fusion.3
  406.5 19.8 %collective-permute-done.14 = bf16[32,32,512]{2,1,0:T(8,128)(2,1)S(1)} collective-permute-done((bf16[32,32,512]{2,1,0:T(8,128)(2,1)S(1)}, bf16[32,32,512]{2,1,0:T(8,128)(2,1)S(1)}, u32[]{:S(2)}, u32[]{:S(2)}) %collective-permute-start.14) | collective-permute-done | bytes 1048608 | tf_op jit(solution)/shard_map/ppermute | solution.py:17
  426.3 1.7 convert_add_fusion.4
  (71 shorter events, 29.7 us)
Async XLA Ops:
  1.9 8.8 %copy-start = (bf16[512,4096]{1,0:T(8,128)(2,1)S(1)}, bf16[512,4096]{1,0:T(8,128)(2,1)}, u32[]{:S(2)}) copy-start(bf16[512,4096]{1,0:T(8,128)(2,1)} %c_ref.5) | copy-start | bytes 12582916
  1.9 23.8 %collective-permute-start.2 = (bf16[16,128,128]{2,1,0:T(8,128)(2,1)S(1)}, bf16[16,128,128]{2,1,0:T(8,128)(2,1)}, u32[]{:S(2)}, u32[]{:S(2)}) collective-permute-start(bf16[16,128,128]{2,1,0:T(8,128)(2,1)S(1)} %dynamic-slice_bitcast_fusion.4), channel_id=1, source_target_pairs={{0,4},{4,0},{8,12},{12,8},{1,5},{5,1},{9,13},{13,9},{2,6},{6,2},{1... | collective-permute-start | bytes 1572872 | tf_op jit(solution)/shard_map/ppermute | solution.py:17
  8.1 49.8 %collective-permute-start = (bf16[128,4096]{1,0:T(8,128)(2,1)}, bf16[128,4096]{1,0:T(8,128)(2,1)}, u32[]{:S(2)}, u32[]{:S(2)}) collective-permute-start(bf16[128,4096]{1,0:T(8,128)(2,1)} %get-tuple-element.47), channel_id=1, source_target_pairs={{0,8},{4,12},{8,0},{12,4},{1,9},{5,13},{9,1},{13,5},{2,10},{6,14},... | collective-permute-start | bytes 3145736 | tf_op jit(solution)/shard_map/ppermute | solution.py:17
  12.2 58.5 %collective-permute-start.1 = (bf16[128,4096]{1,0:T(8,128)(2,1)}, bf16[128,4096]{1,0:T(8,128)(2,1)}, u32[]{:S(2)}, u32[]{:S(2)}) collective-permute-start(bf16[128,4096]{1,0:T(8,128)(2,1)} %get-tuple-element.45), channel_id=1, source_target_pairs={{0,4},{4,0},{8,12},{12,8},{1,5},{5,1},{9,13},{13,9},{2,6},{6,2},{1... | collective-permute-start | bytes 3145736 | tf_op jit(solution)/shard_map/ppermute | solution.py:17
  25.7 7.6 %collective-permute-start.3 = (bf16[16,128,128]{2,1,0:T(8,128)(2,1)}, bf16[16,128,128]{2,1,0:T(8,128)(2,1)}, u32[]{:S(2)}, u32[]{:S(2)}) collective-permute-start(bf16[16,128,128]{2,1,0:T(8,128)(2,1)} %collective-permute-done.2), channel_id=1, source_target_pairs={{0,1},{1,0},{2,3},{3,2},{4,5},{5,4},{6,7},{7,6},{8,9},{9,8},{10,11... | collective-permute-start | bytes 1572872 | tf_op jit(solution)/shard_map/ppermute | solution.py:17
  25.7 80.0 %collective-permute-start.5 = (bf16[128,4096]{1,0:T(8,128)(2,1)}, bf16[128,4096]{1,0:T(8,128)(2,1)S(1)}, u32[]{:S(2)}, u32[]{:S(2)}) collective-permute-start(bf16[128,4096]{1,0:T(8,128)(2,1)} %get-tuple-element.48), channel_id=1, source_target_pairs={{0,8},{4,12},{8,0},{12,4},{1,9},{5,13},{9,1},{13,5},{2,10},{6,14},... | collective-permute-start | bytes 3145736 | tf_op jit(solution)/shard_map/ppermute | solution.py:17
  26.5 134.1 %collective-permute-start.6 = (bf16[128,4096]{1,0:T(8,128)(2,1)}, bf16[128,4096]{1,0:T(8,128)(2,1)}, u32[]{:S(2)}, u32[]{:S(2)}) collective-permute-start(bf16[128,4096]{1,0:T(8,128)(2,1)} %get-tuple-element.46), channel_id=1, source_target_pairs={{0,4},{4,0},{8,12},{12,8},{1,5},{5,1},{9,13},{13,9},{2,6},{6,2},{1... | collective-permute-start | bytes 3145736 | tf_op jit(solution)/shard_map/ppermute | solution.py:17
  33.4 171.3 %collective-permute-start.9 = (bf16[256,4096]{1,0:T(8,128)(2,1)}, bf16[256,4096]{1,0:T(8,128)(2,1)}, u32[]{:S(2)}, u32[]{:S(2)}) collective-permute-start(bf16[256,4096]{1,0:T(8,128)(2,1)} %slice.34), channel_id=1, source_target_pairs={{0,4},{4,0},{8,12},{12,8},{1,5},{5,1},{9,13},{13,9},{2,6},{6,2},{1... | collective-permute-start | bytes 6291464 | tf_op jit(solution)/shard_map/ppermute | solution.py:17
  57.9 146.7 %collective-permute-start.8 = (bf16[256,4096]{1,0:T(8,128)(2,1)S(1)}, bf16[256,4096]{1,0:T(8,128)(2,1)}, u32[]{:S(2)}, u32[]{:S(2)}) collective-permute-start(bf16[256,4096]{1,0:T(8,128)(2,1)S(1)} %slice.33), channel_id=1, source_target_pairs={{0,8},{4,12},{8,0},{12,4},{1,9},{5,13},{9,1},{13,5},{2,10},{6,14},... | collective-permute-start | bytes 6291464 | tf_op jit(solution)/shard_map/ppermute | solution.py:17
  104.8 200.2 %collective-permute-start.4 = (bf16[128,4096]{1,0:T(8,128)(2,1)}, bf16[128,4096]{1,0:T(8,128)(2,1)}, u32[]{:S(2)}, u32[]{:S(2)}) collective-permute-start(bf16[128,4096]{1,0:T(8,128)(2,1)} %get-tuple-element.24), channel_id=1, source_target_pairs={{0,8},{4,12},{8,0},{12,4},{1,9},{5,13},{9,1},{13,5},{2,10},{6,14},... | collective-permute-start | bytes 3145736 | tf_op jit(solution)/shard_map/ppermute | solution.py:17
  105.8 54.8 %copy-start.7 = (bf16[128,4096]{1,0:T(8,128)(2,1)}, bf16[128,4096]{1,0:T(8,128)(2,1)S(1)}, u32[]{:S(2)}) copy-start(bf16[128,4096]{1,0:T(8,128)(2,1)S(1)} %collective-permute-done.5.xf_ref) | copy-start | bytes 3145732
  197.0 130.5 %collective-permute-start.7 = (bf16[128,4096]{1,0:T(8,128)(2,1)}, bf16[128,4096]{1,0:T(8,128)(2,1)S(1)}, u32[]{:S(2)}, u32[]{:S(2)}) collective-permute-start(bf16[128,4096]{1,0:T(8,128)(2,1)} %get-tuple-element.30), channel_id=1, source_target_pairs={{0,8},{4,12},{8,0},{12,4},{1,9},{5,13},{9,1},{13,5},{2,10},{6,14},... | collective-permute-start | bytes 3145736 | tf_op jit(solution)/shard_map/ppermute | solution.py:17
  245.8 136.0 %collective-permute-start.10 = (bf16[256,4096]{1,0:T(8,128)(2,1)}, bf16[256,4096]{1,0:T(8,128)(2,1)S(1)}, u32[]{:S(2)}, u32[]{:S(2)}) collective-permute-start(bf16[256,4096]{1,0:T(8,128)(2,1)} %get-tuple-element.36), channel_id=1, source_target_pairs={{0,8},{4,12},{8,0},{12,4},{1,9},{5,13},{9,1},{13,5},{2,10},{6,14},... | collective-permute-start | bytes 6291464 | tf_op jit(solution)/shard_map/ppermute | solution.py:17
  250.2 79.0 %collective-permute-start.11 = (bf16[32,2,2,32,128]{4,3,1,0,2:T(8,128)(2,1)S(1)}, bf16[32,2,2,32,128]{4,3,1,0,2:T(8,128)(2,1)S(1)}, u32[]{:S(2)}, u32[]{:S(2)}) collective-permute-start(bf16[32,2,2,32,128]{4,3,1,0,2:T(8,128)(2,1)S(1)} %bitcast.71), channel_id=1, source_target_pairs={{0,1},{1,0},{2,3},{3,2},{4,5},{5,4},{6,7},{7,6},{8,9},{9,8},{10,11... | collective-permute-start | bytes 3145736 | tf_op jit(solution)/shard_map/ppermute | solution.py:17
  250.3 56.3 %collective-permute-start.17 = (bf16[32,2,2,32,128]{4,3,0,1,2:T(8,128)(2,1)S(1)}, bf16[32,2,2,32,128]{4,3,0,1,2:T(8,128)(2,1)S(1)}, u32[]{:S(2)}, u32[]{:S(2)}) collective-permute-start(bf16[32,2,2,32,128]{4,3,0,1,2:T(8,128)(2,1)S(1)} %bitcast.72), channel_id=1, source_target_pairs={{0,1},{1,0},{2,3},{3,2},{4,5},{5,4},{6,7},{7,6},{8,9},{9,8},{10,11... | collective-permute-start | bytes 3145736 | tf_op jit(solution)/shard_map/ppermute | solution.py:17
  255.2 49.9 %copy-start.6 = (f32[128,4096]{1,0:T(8,128)S(1)}, f32[128,4096]{1,0:T(8,128)}, u32[]{:S(2)}) copy-start(f32[128,4096]{1,0:T(8,128)} %get-tuple-element.23) | copy-start | bytes 6291460
  305.1 72.7 %collective-permute-start.15 = (bf16[32,2,128,128]{3,2,0,1:T(8,128)(2,1)S(1)}, bf16[32,2,128,128]{3,2,0,1:T(8,128)(2,1)S(1)}, u32[]{:S(2)}, u32[]{:S(2)}) collective-permute-start(bf16[32,2,128,128]{3,2,0,1:T(8,128)(2,1)S(1)} %bitcast.70), channel_id=1, source_target_pairs={{0,1},{1,0},{2,3},{3,2},{4,5},{5,4},{6,7},{7,6},{8,9},{9,8},{10,11... | collective-permute-start | bytes 6291464 | tf_op jit(solution)/shard_map/ppermute | solution.py:17
  306.6 73.7 %collective-permute-start.13 = (bf16[32,2,32,512]{3,2,0,1:T(8,128)(2,1)S(1)}, bf16[32,2,32,512]{3,2,0,1:T(8,128)(2,1)S(1)}, u32[]{:S(2)}, u32[]{:S(2)}) collective-permute-start(bf16[32,2,32,512]{3,2,0,1:T(8,128)(2,1)S(1)} %bitcast.69), channel_id=1, source_target_pairs={{0,1},{1,0},{2,3},{3,2},{4,5},{5,4},{6,7},{7,6},{8,9},{9,8},{10,11... | collective-permute-start | bytes 6291464 | tf_op jit(solution)/shard_map/ppermute | solution.py:17
  307.2 21.8 %copy-start.5 = (f32[128,4096]{1,0:T(8,128)S(1)}, f32[128,4096]{1,0:T(8,128)}, u32[]{:S(2)}) copy-start(f32[128,4096]{1,0:T(8,128)} %get-tuple-element.29) | copy-start | bytes 6291460
  327.5 14.8 %collective-permute-start.18 = (bf16[32,2,32,128]{3,2,0,1:T(8,128)(2,1)S(1)}, bf16[32,2,32,128]{3,2,0,1:T(8,128)(2,1)S(1)}, u32[]{:S(2)}, u32[]{:S(2)}) collective-permute-start(bf16[32,2,32,128]{3,2,0,1:T(8,128)(2,1)S(1)} %dynamic-slice_bitcast_fusion.2), channel_id=1, source_target_pairs={{0,2},{2,0},{1,3},{3,1},{4,6},{6,4},{5,7},{7,5},{8,10},{10,8},{9,1... | collective-permute-start | bytes 1572872 | tf_op jit(solution)/shard_map/ppermute | solution.py:17
  329.6 20.3 %collective-permute-start.12 = (bf16[32,2,32,128]{3,2,1,0:T(8,128)(2,1)S(1)}, bf16[32,2,32,128]{3,2,1,0:T(8,128)(2,1)S(1)}, u32[]{:S(2)}, u32[]{:S(2)}) collective-permute-start(bf16[32,2,32,128]{3,2,1,0:T(8,128)(2,1)S(1)} %dynamic-slice_bitcast_fusion.3), channel_id=1, source_target_pairs={{0,2},{2,0},{1,3},{3,1},{4,6},{6,4},{5,7},{7,5},{8,10},{10,8},{9,1... | collective-permute-start | bytes 1572872 | tf_op jit(solution)/shard_map/ppermute | solution.py:17
  342.5 34.2 %collective-permute-start.19 = (bf16[32,32,128]{2,1,0:T(8,128)(2,1)S(1)}, bf16[32,32,128]{2,1,0:T(8,128)(2,1)S(1)}, u32[]{:S(2)}, u32[]{:S(2)}) collective-permute-start(bf16[32,32,128]{2,1,0:T(8,128)(2,1)S(1)} %fusion.4), channel_id=1, source_target_pairs={{0,4},{4,0},{8,12},{12,8},{1,5},{5,1},{9,13},{13,9},{2,6},{6,2},{1... | collective-permute-start | bytes 786440 | tf_op jit(solution)/shard_map/ppermute | solution.py:17
  378.7 26.1 %collective-permute-start.16 = (bf16[32,128,128]{2,1,0:T(8,128)(2,1)S(1)}, bf16[32,128,128]{2,1,0:T(8,128)(2,1)S(1)}, u32[]{:S(2)}, u32[]{:S(2)}) collective-permute-start(bf16[32,128,128]{2,1,0:T(8,128)(2,1)S(1)} %dynamic-slice_bitcast_fusion), channel_id=1, source_target_pairs={{0,2},{2,0},{1,3},{3,1},{4,6},{6,4},{5,7},{7,5},{8,10},{10,8},{9,1... | collective-permute-start | bytes 3145736 | tf_op jit(solution)/shard_map/ppermute | solution.py:17
  381.2 45.1 %collective-permute-start.14 = (bf16[32,32,512]{2,1,0:T(8,128)(2,1)S(1)}, bf16[32,32,512]{2,1,0:T(8,128)(2,1)S(1)}, u32[]{:S(2)}, u32[]{:S(2)}) collective-permute-start(bf16[32,32,512]{2,1,0:T(8,128)(2,1)S(1)} %dynamic-slice_bitcast_fusion.1), channel_id=1, source_target_pairs={{0,2},{2,0},{1,3},{3,1},{4,6},{6,4},{5,7},{7,5},{8,10},{10,8},{9,1... | collective-permute-start | bytes 3145736 | tf_op jit(solution)/shard_map/ppermute | solution.py:17
  (5 other events, 10.6 us)
where the time goes:
time: 431 us; the launch traced here: 428 us
  waiting for transfers between devices  263 us (61%)
  Pallas kernels  112 us (26%)
  local copies, waits for them, and re-layouts  19.4 us (5%)
  starting transfers between devices  17.7 us (4%)
  other arithmetic  15 us (3%)
    ppermute x20, waiting for transfers between devices, swapped(): lax.ppermute(x, axis, [(i, i ^ 1 << bit) for i in range(lax.axis_size(axi...  263 us
    pallas_call x3, Pallas kernels, process(): pl.pallas_call(functools.partial(block_kernel, prev is not None), grid_sp...  112 us
    ppermute x20, starting transfers between devices, swapped(): lax.ppermute(x, axis, [(i, i ^ 1 << bit) for i in range(lax.axis_size(axi...  17.7 us
  transfers between devices with their start and end apart: 20, of which 12 were waited for; matrix products, arithmetic and copies ran while one was open for 6% of the time, Pallas kernels for 26%

commit v1 on v0

--- a/solution.py
+++ b/solution.py
@@ -151,14 +151,45 @@
 
 
 def neighbour_weights(weights):
-    half = weights.shape[0] // 2
-    side = lax.axis_index("rep")
-    part = lax.dynamic_slice_in_dim(weights, side * half, half, axis=0)
+    quarter = weights.shape[0] // 4
+    rep = lax.axis_index("rep") & 1
+    dp = lax.axis_index("dp") & 1
+    part = lax.dynamic_slice_in_dim(weights, (dp * 2 + rep) * quarter, quarter, axis=0)
     mine = swapped(part, "feat", 0)
-    other = swapped(mine, "rep", 0)
-    low = jnp.where(side == 0, mine, other)
-    high = jnp.where(side == 0, other, mine)
-    return jnp.concatenate([low, high], axis=0)
+    for side, axis in ((rep, "rep"), (dp, "dp")):
+        other = swapped(mine, axis, 0)
+        low = jnp.where(side == 0, mine, other)
+        high = jnp.where(side == 0, other, mine)
+        mine = jnp.concatenate([low, high], axis=0)
+    return mine
+
+
+def finish_kernel(direct_ref, back_ref, *rest):
+    rest[-1][...] = (direct_ref[...] + back_ref[...].astype(jnp.float32)).astype(jnp.bfloat16)
+
+
+def finish(offset, total, direct, back, held):
+    rows, columns = direct.shape
+    tile = rows // 2
+    spec = pl.BlockSpec((tile, columns // 4), lambda i, j: (i, j))
+    operands = [direct, back]
+    in_specs = [spec, spec]
+    aliases = {}
+    if held is not None:
+        operands.append(held)
+        in_specs.append(pl.BlockSpec(memory_space=pl.ANY))
+        aliases = {2: 0}
+    return pl.pallas_call(
+        finish_kernel,
+        grid=(2, 4),
+        in_specs=in_specs,
+        out_specs=pl.BlockSpec((tile, columns // 4), lambda i, j: (offset // tile + i, j)),
+        out_shape=jax.ShapeDtypeStruct((total, columns), jnp.bfloat16),
+        input_output_aliases=aliases,
+        cost_estimate=pl.CostEstimate(
+            flops=rows * columns, bytes_accessed=8 * rows * columns, transcendentals=0
+        ),
+    )(*operands)
 
 
 def per_device(tokens, cotangent, mix_first, up_weight, down_weight, mix_second, order):
@@ -188,13 +219,9 @@
     up_sum = summed(up, 1)
     down_sum = summed(down, 1)
     first_sum = summed(first, 2)
-    grad_inputs = jnp.concatenate(
-        [
-            (direct + back.astype(jnp.float32)).astype(jnp.bfloat16)
-            for direct, back in zip(directs, backs)
-        ],
-        axis=0,
-    )
+    grad_inputs = None
+    for offset, direct, back in zip(offsets, directs, backs):
+        grad_inputs = finish(offset, row_count, direct, back, grad_inputs)
     return grad_inputs, first_sum, up_sum, down_sum, second_sum
 
 

time: 431 us -> 446 us (1.035)
  waiting for transfers between devices: 263 us -> 237 us
  Pallas kernels: 112 us -> 129 us
  starting transfers between devices: 17.7 us -> 30.6 us
  local copies, waits for them, and re-layouts: 19.4 us -> 26.3 us
    ppermute x20 -> x21, waiting for transfers between devices: 263 us -> 237 us  [swapped(): lax.ppermute(x, axis, [(i, i ^ 1 << bit) for i in range(lax.axis_size(axi...]
    pallas_call x0 -> x3, Pallas kernels: none -> 17.9 us  [finish(): pl.pallas_call(finish_kernel, grid=(2, 4), in_specs=in_specs, out_specs=p...]
    ppermute x20 -> x21, starting transfers between devices: 17.7 us -> 30.6 us  [swapped(): lax.ppermute(x, axis, [(i, i ^ 1 << bit) for i in range(lax.axis_size(axi...]
    convert_element_type x4, other arithmetic: 2.27 us -> 8.27 us  [summed(): x = x.astype(jnp.bfloat16)]
  transfers between devices with their start and end apart: 20 -> 21, of which waited for: 12 -> 12; matrix products, arithmetic and copies ran while one was open for 6% -> 7% of each run, Pallas kernels for 26% -> 20%
where the time goes in v1:
time: 446 us; the launch traced here: 442 us
  waiting for transfers between devices  237 us (53%)
  Pallas kernels  129 us (29%)
  starting transfers between devices  30.6 us (7%)
  local copies, waits for them, and re-layouts  26.3 us (6%)
  other arithmetic  18.4 us (4%)
    ppermute x21, waiting for transfers between devices, swapped(): lax.ppermute(x, axis, [(i, i ^ 1 << bit) for i in range(lax.axis_size(axi...  237 us
    pallas_call x3, Pallas kernels, process(): pl.pallas_call(functools.partial(block_kernel, prev is not None), grid_sp...  112 us
    ppermute x21, starting transfers between devices, swapped(): lax.ppermute(x, axis, [(i, i ^ 1 << bit) for i in range(lax.axis_size(axi...  30.6 us
    pallas_call x3, Pallas kernels, finish(): pl.pallas_call(finish_kernel, grid=(2, 4), in_specs=in_specs, out_specs=p...  17.9 us
  transfers between devices with their start and end apart: 21, of which 12 were waited for; matrix products, arithmetic and copies ran while one was open for 7% of the time, Pallas kernels for 20%

profile of v1, /device:TPU:0, one launch (start us, length us, event | category | flops | bytes accessed | tf_op | source)
XLA Modules:
  0.0 442.3 jit_solution(2206453973113082905)
XLA Ops:
  1.9 3.1 collective-permute-start.2
  5.0 3.1 fusion.6
  16.9 3.6 collective-permute-start.5
  21.1 3.3 slice.28
  24.5 5.2 %collective-permute-done.4 = bf16[16,128,128]{2,1,0:T(8,128)(2,1)S(1)} collective-permute-done((bf16[16,128,128]{2,1,0:T(8,128)(2,1)}, bf16[16,128,128]{2,1,0:T(8,128)(2,1)S(1)}, u32[]{:S(2)}, u32[]{:S(2)}) %collective-permute-start.4) | collective-permute-done | bytes 524320 | tf_op jit(solution)/shard_map/ppermute | solution.py:17
  29.7 3.6 collective-permute-start
  33.3 24.6 %collective-permute-done.7.xf_ref = bf16[128,4096]{1,0:T(8,128)(2,1)} collective-permute-done((bf16[128,4096]{1,0:T(8,128)(2,1)}, bf16[128,4096]{1,0:T(8,128)(2,1)}, u32[]{:S(2)}, u32[]{:S(2)}) %collective-permute-start.7) | collective-permute-done | bytes 1048608 | tf_op jit(solution)/shard_map/ppermute | solution.py:17
  61.6 34.2 %shard_map.110 = (bf16[128,4096]{1,0:T(8,128)(2,1)}, f32[128,4096]{1,0:T(8,128)}, bf16[32,2,128,128]{3,2,1,0:T(8,128)(2,1)}, bf16[32,128,512]{2,1,0:T(8,128)(2,1...) custom-call(s32[32]{0:T(128)} %order_ref.5, bf16[512,4096]{1,0:T(8,128)(2,1)} %x_ref.5, ...), custom_call_target="tpu_custom_call" | custom-call | flops 9126805504 | bytes 62914560 | tf_op jit(solution)/shard_map/pallas_call | solution.py:109
  95.8 7.0 %collective-permute-done.5.xf_ref = bf16[128,4096]{1,0:T(8,128)(2,1)} collective-permute-done((bf16[128,4096]{1,0:T(8,128)(2,1)}, bf16[128,4096]{1,0:T(8,128)(2,1)}, u32[]{:S(2)}, u32[]{:S(2)}) %collective-permute-start.5) | collective-permute-done | bytes 1048608 | tf_op jit(solution)/shard_map/ppermute | solution.py:17
  102.8 3.7 collective-permute-done.6.cn_ref
  106.6 36.4 %shard_map.111 = (bf16[128,4096]{1,0:T(8,128)(2,1)}, f32[128,4096]{1,0:T(8,128)}, bf16[32,2,128,128]{3,2,1,0:T(8,128)(2,1)}, bf16[32,128,512]{2,1,0:T(8,128)(2,1...) custom-call(s32[32]{0:T(128)} %order_ref.5, bf16[512,4096]{1,0:T(8,128)(2,1)} %x_ref.5, ...), custom_call_target="tpu_custom_call" | custom-call | flops 9126805504 | bytes 62914560 | tf_op jit(solution)/shard_map/pallas_call | solution.py:109
  142.9 48.5 %collective-permute-done.xf_ref = bf16[256,4096]{1,0:T(8,128)(2,1)} collective-permute-done((bf16[256,4096]{1,0:T(8,128)(2,1)}, bf16[256,4096]{1,0:T(8,128)(2,1)}, u32[]{:S(2)}, u32[]{:S(2)}) %collective-permute-start) | collective-permute-done | bytes 2097184 | tf_op jit(solution)/shard_map/ppermute | solution.py:17
  193.7 41.1 %shard_map.112 = (bf16[256,4096]{1,0:T(8,128)(2,1)}, f32[256,4096]{1,0:T(8,128)}, bf16[32,2,128,128]{3,2,1,0:T(8,128)(2,1)}, bf16[32,128,512]{2,1,0:T(8,128)(2,1...) custom-call(s32[32]{0:T(128)} %order_ref.5, bf16[512,4096]{1,0:T(8,128)(2,1)} %x_ref.5, ...), custom_call_target="tpu_custom_call" | custom-call | flops 18253611008 | bytes 62914560 | tf_op jit(solution)/shard_map/pallas_call | solution.py:109
  234.9 4.8 %constant_dynamic-slice_fusion.1 = (bf16[32,2,2,1,32,128]{5,4,3,2,1,0:T(8,128)(2,1)}, bf16[32,2,2,1,32,128]{5,4,3,2,1,0:T(8,128)(2,1)S(1)}, bf16[32,2,2,1,32,128...) fusion(bf16[32,2,2,2,32,128]{5,4,3,2,1,0:T(8,128)(2,1)} %bitcast.68, s32[]{:T(128)S(6)} %select_n.64, ...), kind=kLoop, calls=%fused_computation.37 | loop fusion | bytes 8388616 | tf_op jit(solution)/shard_map/jit(dynamic_index_in_dim)/dynamic_slice | solution.py:144
  242.4 4.0 collective-permute-start.11
  254.9 60.8 %collective-permute-done.11.back_ref = bf16[128,4096]{1,0:T(8,128)(2,1)} collective-permute-done((bf16[128,4096]{1,0:T(8,128)(2,1)}, bf16[128,4096]{1,0:T(8,128)(2,1)}, u32[]{:S(2)}, u32[]{:S(2)}) %collective-permute-start.11) | collective-permute-done | bytes 1048608 | tf_op jit(solution)/shard_map/ppermute | solution.py:17
  317.3 5.6 %shard_map.113.rest_0_ = bf16[512,4096]{1,0:T(8,128)(2,1)} custom-call(f32[128,4096]{1,0:T(8,128)} %get-tuple-element.35.direct_ref, bf16[128,4096]{1,0:T(8,128)(2,1)} %collective-permute-done.11.back_ref), custom_call_target="tpu_custom_call" | custom-call | flops 524288 | bytes 4194304 | tf_op jit(solution)/shard_map/pallas_call | solution.py:182
  322.9 14.5 %collective-permute-done.10.back_ref = bf16[128,4096]{1,0:T(8,128)(2,1)} collective-permute-done((bf16[128,4096]{1,0:T(8,128)(2,1)}, bf16[128,4096]{1,0:T(8,128)(2,1)}, u32[]{:S(2)}, u32[]{:S(2)}) %collective-permute-start.10) | collective-permute-done | bytes 1048608 | tf_op jit(solution)/shard_map/ppermute | solution.py:17
  337.4 5.6 %shard_map.114.rest_0_ = bf16[512,4096]{1,0:T(8,128)(2,1)} custom-call(f32[128,4096]{1,0:T(8,128)} %get-tuple-element.33.direct_ref, bf16[128,4096]{1,0:T(8,128)(2,1)} %collective-permute-done.10.back_ref, bf16[512,4096]{1,0:T(8,128)(2,1)} %shard_map.113.rest_0_), custom_call_target="tpu_custom_call", output_to_operand_aliasing={{}: (2, {})} | custom-call | flops 524288 | bytes 4194304 | tf_op jit(solution)/shard_map/pallas_call | solution.py:182
  357.0 4.2 collective-permute-start.20
  362.3 25.8 %collective-permute-done.20 = bf16[32,32,128]{2,1,0:T(8,128)(2,1)S(1)} collective-permute-done((bf16[32,32,128]{2,1,0:T(8,128)(2,1)S(1)}, bf16[32,32,128]{2,1,0:T(8,128)(2,1)S(1)}, u32[]{:S(2)}, u32[]{:S(2)}) %collective-permute-start.20) | collective-permute-done | bytes 262176 | tf_op jit(solution)/shard_map/ppermute | solution.py:17
  389.2 41.4 %collective-permute-done.9.back_ref = bf16[256,4096]{1,0:T(8,128)(2,1)} collective-permute-done((bf16[256,4096]{1,0:T(8,128)(2,1)}, bf16[256,4096]{1,0:T(8,128)(2,1)}, u32[]{:S(2)}, u32[]{:S(2)}) %collective-permute-start.9) | collective-permute-done | bytes 2097184 | tf_op jit(solution)/shard_map/ppermute | solution.py:17
  430.6 6.7 %shard_map.115 = bf16[512,4096]{1,0:T(8,128)(2,1)} custom-call(f32[256,4096]{1,0:T(8,128)} %get-tuple-element.31.direct_ref, bf16[256,4096]{1,0:T(8,128)(2,1)} %collective-permute-done.9.back_ref, bf16[512,4096]{1,0:T(8,128)(2,1)} %shard_map.114.rest_0_), custom_call_target="tpu_custom_call", output_to_operand_aliasing={{}: (2, {})} | custom-call | flops 1048576 | bytes 8388608 | tf_op jit(solution)/shard_map/pallas_call | solution.py:182
  439.4 2.9 convert_add_fusion.4
  (80 shorter events, 48.1 us)
Async XLA Ops:
  1.9 9.4 %copy-start = (bf16[512,4096]{1,0:T(8,128)(2,1)S(1)}, bf16[512,4096]{1,0:T(8,128)(2,1)}, u32[]{:S(2)}) copy-start(bf16[512,4096]{1,0:T(8,128)(2,1)} %c_ref.5) | copy-start | bytes 12582916
  1.9 9.4 %collective-permute-start.2 = (bf16[8,128,128]{2,1,0:T(8,128)(2,1)S(1)}, bf16[8,128,128]{2,1,0:T(8,128)(2,1)S(1)}, u32[]{:S(2)}, u32[]{:S(2)}) collective-permute-start(bf16[8,128,128]{2,1,0:T(8,128)(2,1)S(1)} %dynamic-slice_bitcast_fusion.4), channel_id=1, source_target_pairs={{0,4},{4,0},{8,12},{12,8},{1,5},{5,1},{9,13},{13,9},{2,6},{6,2},{1... | collective-permute-start | bytes 786440 | tf_op jit(solution)/shard_map/ppermute | solution.py:17
  8.1 49.8 %collective-permute-start.7 = (bf16[128,4096]{1,0:T(8,128)(2,1)}, bf16[128,4096]{1,0:T(8,128)(2,1)}, u32[]{:S(2)}, u32[]{:S(2)}) collective-permute-start(bf16[128,4096]{1,0:T(8,128)(2,1)} %get-tuple-element.47), channel_id=1, source_target_pairs={{0,8},{4,12},{8,0},{12,4},{1,9},{5,13},{9,1},{13,5},{2,10},{6,14},... | collective-permute-start | bytes 3145736 | tf_op jit(solution)/shard_map/ppermute | solution.py:17
  11.3 3.2 collective-permute-start.3
  12.8 48.8 %collective-permute-start.8 = (bf16[128,4096]{1,0:T(8,128)(2,1)}, bf16[128,4096]{1,0:T(8,128)(2,1)}, u32[]{:S(2)}, u32[]{:S(2)}) collective-permute-start(bf16[128,4096]{1,0:T(8,128)(2,1)} %get-tuple-element.45), channel_id=1, source_target_pairs={{0,4},{4,0},{8,12},{12,8},{1,5},{5,1},{9,13},{13,9},{2,6},{6,2},{1... | collective-permute-start | bytes 3145736 | tf_op jit(solution)/shard_map/ppermute | solution.py:17
  15.4 14.3 %collective-permute-start.4 = (bf16[16,128,128]{2,1,0:T(8,128)(2,1)}, bf16[16,128,128]{2,1,0:T(8,128)(2,1)S(1)}, u32[]{:S(2)}, u32[]{:S(2)}) collective-permute-start(bf16[16,128,128]{2,1,0:T(8,128)(2,1)} %pad_maximum_fusion.2), channel_id=1, source_target_pairs={{0,2},{2,0},{1,3},{3,1},{4,6},{6,4},{5,7},{7,5},{8,10},{10,8},{9,1... | collective-permute-start | bytes 1572872 | tf_op jit(solution)/shard_map/ppermute | solution.py:17
  16.9 85.9 %collective-permute-start.5 = (bf16[128,4096]{1,0:T(8,128)(2,1)}, bf16[128,4096]{1,0:T(8,128)(2,1)}, u32[]{:S(2)}, u32[]{:S(2)}) collective-permute-start(bf16[128,4096]{1,0:T(8,128)(2,1)} %get-tuple-element.48), channel_id=1, source_target_pairs={{0,8},{4,12},{8,0},{12,4},{1,9},{5,13},{9,1},{13,5},{2,10},{6,14},... | collective-permute-start | bytes 3145736 | tf_op jit(solution)/shard_map/ppermute | solution.py:17
  20.5 86.1 %collective-permute-start.6 = (bf16[128,4096]{1,0:T(8,128)(2,1)}, bf16[128,4096]{1,0:T(8,128)(2,1)}, u32[]{:S(2)}, u32[]{:S(2)}) collective-permute-start(bf16[128,4096]{1,0:T(8,128)(2,1)} %get-tuple-element.46), channel_id=1, source_target_pairs={{0,4},{4,0},{8,12},{12,8},{1,5},{5,1},{9,13},{13,9},{2,6},{6,2},{1... | collective-permute-start | bytes 3145736 | tf_op jit(solution)/shard_map/ppermute | solution.py:17
  29.7 161.7 %collective-permute-start = (bf16[256,4096]{1,0:T(8,128)(2,1)}, bf16[256,4096]{1,0:T(8,128)(2,1)}, u32[]{:S(2)}, u32[]{:S(2)}) collective-permute-start(bf16[256,4096]{1,0:T(8,128)(2,1)} %slice.28), channel_id=1, source_target_pairs={{0,8},{4,12},{8,0},{12,4},{1,9},{5,13},{9,1},{13,5},{2,10},{6,14},... | collective-permute-start | bytes 6291464 | tf_op jit(solution)/shard_map/ppermute | solution.py:17
  57.8 135.9 %collective-permute-start.1 = (bf16[256,4096]{1,0:T(8,128)(2,1)S(1)}, bf16[256,4096]{1,0:T(8,128)(2,1)}, u32[]{:S(2)}, u32[]{:S(2)}) collective-permute-start(bf16[256,4096]{1,0:T(8,128)(2,1)S(1)} %slice.29), channel_id=1, source_target_pairs={{0,4},{4,0},{8,12},{12,8},{1,5},{5,1},{9,13},{13,9},{2,6},{6,2},{1... | collective-permute-start | bytes 6291464 | tf_op jit(solution)/shard_map/ppermute | solution.py:17
  239.7 11.0 %collective-permute-start.18 = (bf16[32,2,2,32,128]{4,3,0,1,2:T(8,128)(2,1)S(1)}, bf16[32,2,2,32,128]{4,3,0,1,2:T(8,128)(2,1)}, u32[]{:S(2)}, u32[]{:S(2)}) collective-permute-start(bf16[32,2,2,32,128]{4,3,0,1,2:T(8,128)(2,1)S(1)} %bitcast.69), channel_id=1, source_target_pairs={{0,1},{1,0},{2,3},{3,2},{4,5},{5,4},{6,7},{7,6},{8,9},{9,8},{10,11... | collective-permute-start | bytes 3145736 | tf_op jit(solution)/shard_map/ppermute | solution.py:17
  240.2 7.3 %copy-start.9 = (bf16[32,128,512]{2,1,0:T(8,128)(2,1)S(1)}, bf16[32,128,512]{2,1,0:T(8,128)(2,1)}, u32[]{:S(2)}) copy-start(bf16[32,128,512]{2,1,0:T(8,128)(2,1)} %get-tuple-element.38) | copy-start | bytes 12582916
  241.9 105.7 %collective-permute-start.16 = (bf16[32,2,128,128]{3,2,0,1:T(8,128)(2,1)}, bf16[32,2,128,128]{3,2,0,1:T(8,128)(2,1)}, u32[]{:S(2)}, u32[]{:S(2)}) collective-permute-start(bf16[32,2,128,128]{3,2,0,1:T(8,128)(2,1)} %bitcast.61), channel_id=1, source_target_pairs={{0,1},{1,0},{2,3},{3,2},{4,5},{5,4},{6,7},{7,6},{8,9},{9,8},{10,11... | collective-permute-start | bytes 6291464 | tf_op jit(solution)/shard_map/ppermute | solution.py:17
  242.4 73.3 %collective-permute-start.11 = (bf16[128,4096]{1,0:T(8,128)(2,1)}, bf16[128,4096]{1,0:T(8,128)(2,1)}, u32[]{:S(2)}, u32[]{:S(2)}) collective-permute-start(bf16[128,4096]{1,0:T(8,128)(2,1)} %get-tuple-element.36), channel_id=1, source_target_pairs={{0,8},{4,12},{8,0},{12,4},{1,9},{5,13},{9,1},{13,5},{2,10},{6,14},... | collective-permute-start | bytes 3145736 | tf_op jit(solution)/shard_map/ppermute | solution.py:17
  246.4 91.1 %collective-permute-start.10 = (bf16[128,4096]{1,0:T(8,128)(2,1)}, bf16[128,4096]{1,0:T(8,128)(2,1)}, u32[]{:S(2)}, u32[]{:S(2)}) collective-permute-start(bf16[128,4096]{1,0:T(8,128)(2,1)} %get-tuple-element.34), channel_id=1, source_target_pairs={{0,8},{4,12},{8,0},{12,4},{1,9},{5,13},{9,1},{13,5},{2,10},{6,14},... | collective-permute-start | bytes 3145736 | tf_op jit(solution)/shard_map/ppermute | solution.py:17
  247.5 95.5 %collective-permute-start.12 = (bf16[32,2,2,32,128]{4,3,1,0,2:T(8,128)(2,1)}, bf16[32,2,2,32,128]{4,3,1,0,2:T(8,128)(2,1)}, u32[]{:S(2)}, u32[]{:S(2)}) collective-permute-start(bf16[32,2,2,32,128]{4,3,1,0,2:T(8,128)(2,1)} %bitcast.64), channel_id=1, source_target_pairs={{0,1},{1,0},{2,3},{3,2},{4,5},{5,4},{6,7},{7,6},{8,9},{9,8},{10,11... | collective-permute-start | bytes 3145736 | tf_op jit(solution)/shard_map/ppermute | solution.py:17
  250.7 100.9 %collective-permute-start.14 = (bf16[32,2,32,512]{3,2,0,1:T(8,128)(2,1)}, bf16[32,2,32,512]{3,2,0,1:T(8,128)(2,1)}, u32[]{:S(2)}, u32[]{:S(2)}) collective-permute-start(bf16[32,2,32,512]{3,2,0,1:T(8,128)(2,1)} %bitcast.62), channel_id=1, source_target_pairs={{0,1},{1,0},{2,3},{3,2},{4,5},{5,4},{6,7},{7,6},{8,9},{9,8},{10,11... | collective-permute-start | bytes 6291464 | tf_op jit(solution)/shard_map/ppermute | solution.py:17
  315.6 30.7 %collective-permute-start.19 = (bf16[32,2,32,128]{3,2,0,1:T(8,128)(2,1)}, bf16[32,2,32,128]{3,2,0,1:T(8,128)(2,1)}, u32[]{:S(2)}, u32[]{:S(2)}) collective-permute-start(bf16[32,2,32,128]{3,2,0,1:T(8,128)(2,1)} %dynamic-slice_bitcast_fusion.2), channel_id=1, source_target_pairs={{0,2},{2,0},{1,3},{3,1},{4,6},{6,4},{5,7},{7,5},{8,10},{10,8},{9,1... | collective-permute-start | bytes 1572872 | tf_op jit(solution)/shard_map/ppermute | solution.py:17
  337.4 93.1 %collective-permute-start.9 = (bf16[256,4096]{1,0:T(8,128)(2,1)}, bf16[256,4096]{1,0:T(8,128)(2,1)}, u32[]{:S(2)}, u32[]{:S(2)}) collective-permute-start(bf16[256,4096]{1,0:T(8,128)(2,1)} %get-tuple-element.32), channel_id=1, source_target_pairs={{0,8},{4,12},{8,0},{12,4},{1,9},{5,13},{9,1},{13,5},{2,10},{6,14},... | collective-permute-start | bytes 6291464 | tf_op jit(solution)/shard_map/ppermute | solution.py:17
  344.8 16.4 %collective-permute-start.13 = (bf16[32,2,32,128]{3,2,1,0:T(8,128)(2,1)S(1)}, bf16[32,2,32,128]{3,2,1,0:T(8,128)(2,1)S(1)}, u32[]{:S(2)}, u32[]{:S(2)}) collective-permute-start(bf16[32,2,32,128]{3,2,1,0:T(8,128)(2,1)S(1)} %dynamic-slice_bitcast_fusion.3), channel_id=1, source_target_pairs={{0,2},{2,0},{1,3},{3,1},{4,6},{6,4},{5,7},{7,5},{8,10},{10,8},{9,1... | collective-permute-start | bytes 1572872 | tf_op jit(solution)/shard_map/ppermute | solution.py:17
  351.1 86.2 %collective-permute-start.17 = (bf16[32,128,128]{2,1,0:T(8,128)(2,1)}, bf16[32,128,128]{2,1,0:T(8,128)(2,1)S(1)}, u32[]{:S(2)}, u32[]{:S(2)}) collective-permute-start(bf16[32,128,128]{2,1,0:T(8,128)(2,1)} %dynamic-slice_bitcast_fusion), channel_id=1, source_target_pairs={{0,2},{2,0},{1,3},{3,1},{4,6},{6,4},{5,7},{7,5},{8,10},{10,8},{9,1... | collective-permute-start | bytes 3145736 | tf_op jit(solution)/shard_map/ppermute | solution.py:17
  355.1 7.2 %copy-start.5 = (bf16[32,2,32,512]{3,2,0,1:T(8,128)(2,1)}, bf16[32,2,32,512]{3,2,0,1:T(8,128)(2,1)S(1)}, u32[]{:S(2)}) copy-start(bf16[32,2,32,512]{3,2,0,1:T(8,128)(2,1)S(1)} %fusion.1) | copy-start | bytes 6291460
  356.4 82.6 %collective-permute-start.15 = (bf16[32,32,512]{2,1,0:T(8,128)(2,1)}, bf16[32,32,512]{2,1,0:T(8,128)(2,1)}, u32[]{:S(2)}, u32[]{:S(2)}) collective-permute-start(bf16[32,32,512]{2,1,0:T(8,128)(2,1)} %dynamic-slice_bitcast_fusion.1), channel_id=1, source_target_pairs={{0,2},{2,0},{1,3},{3,1},{4,6},{6,4},{5,7},{7,5},{8,10},{10,8},{9,1... | collective-permute-start | bytes 3145736 | tf_op jit(solution)/shard_map/ppermute | solution.py:17
  357.0 31.1 %collective-permute-start.20 = (bf16[32,32,128]{2,1,0:T(8,128)(2,1)S(1)}, bf16[32,32,128]{2,1,0:T(8,128)(2,1)S(1)}, u32[]{:S(2)}, u32[]{:S(2)}) collective-permute-start(bf16[32,32,128]{2,1,0:T(8,128)(2,1)S(1)} %fusion.4), channel_id=1, source_target_pairs={{0,4},{4,0},{8,12},{12,8},{1,5},{5,1},{9,13},{13,9},{2,6},{6,2},{1... | collective-permute-start | bytes 786440 | tf_op jit(solution)/shard_map/ppermute | solution.py:17
  (9 other events, 30.4 us)
